TPU v7x, 32 devices: a whole 2x2x4 slice. The times are simulated.
32 devices in a mesh: row: 8 (over z, x), col: 4 (over y, core).
Axes of the slice: x: 2, y: 2, z: 4, core: 2. Of those that a mesh axis runs over, the one named last changes fastest.
Arguments:
- layer_input: bfloat16 [16384, 960], P(('row', 'col')), may hold values from -6 to 6
- norm1_gain: float32 [960], replicated, may hold values from 0.5 to 1.5
- w_qkv: bfloat16 [960, 1600], P('row', 'col'), may hold values from -0.1875 to 0.1875
- w_out: bfloat16 [960, 960], P('row', 'col'), may hold values from -1.5 to 1.5
- norm2_gain: float32 [960], replicated, may hold values from 0.5 to 1.5
- w_gate: bfloat16 [960, 2560], P('row', 'col'), may hold values from -0.1875 to 0.1875
- w_up: bfloat16 [960, 2560], P('row', 'col'), may hold values from -0.1875 to 0.1875
- w_down: bfloat16 [960, 2560], P('row', 'col'), may hold values from -0.15625 to 0.15625
- out_cotangent: bfloat16 [16384, 960], P(('row', 'col')), may hold values from -6 to 6
- seq_lengths: int32 [8, 3], P('row'), may hold values from 1 to 1024, 2048 in all within a row
- position_ids: int32 [16384], P(('row', 'col')), may hold values from 0 to 4094, as said below
- deal_rows: int32 [32, 8], P(('row', 'col')), may hold values from 0 to 7, each once within a row
Outputs:
- layer_output: bfloat16 [16384, 960], P(('row', 'col'))
- grad_input: bfloat16 [16384, 960], P(('row', 'col'))
- grad_norm1: float32 [960], replicated
- grad_qkv: float32 [960, 1600], P('row', 'col')
- grad_out: float32 [960, 960], P('row', 'col')
- grad_norm2: float32 [960], replicated
- grad_gate: float32 [960, 2560], P('row', 'col')
- grad_up: float32 [960, 2560], P('row', 'col')
- grad_down: float32 [960, 2560], P('row', 'col')
Inputs may be any that keep to these rules, and one draw needn't show every extreme that they name: Each row of seq_lengths gives the lengths of the 3 sequences packed in order into one row group of 2048 dealt rows; each row sums to 2048, and its largest entry is exactly 1024. `position_ids`: within each aligned group of 2048 dealt rows the ids start at 0 and rise by 1 or 2 from one row to the next; in some group they rise by 2 at every row. `deal_rows`: each row is a permutation of the 8 row groups.
All inputs are finite; a program needn't handle non-finite values.
Results may differ from a plain program's by a relative error of at most 0.015.
Values may be sent and summed in bfloat16 or wider, within the bound.
A program may use at most 128 MiB of HBM per device.

v0:
```python
import math
import jax
import jax.numpy as jnp
from jax import lax
from jax.sharding import PartitionSpec as P

QUERY_HEADS = 15
KEY_VALUE_HEADS = 5
HEAD_DIMENSION = 64
QUERY_FEATURES = 960
KEY_FEATURES = 320
EPS = 1e-05
NEG_FILL = -1e30
THETA = 10000.0


def matmul(left_mat, right_mat):
    return jnp.dot(left_mat, right_mat, preferred_element_type=jnp.float32)


def matmul_nt(left_mat, right_mat):
    return lax.dot_general(
        left_mat, right_mat, (((1,), (1,)), ((), ())), preferred_element_type=jnp.float32
    )


def matmul_tn(left_mat, right_mat):
    return lax.dot_general(
        left_mat, right_mat, (((0,), (0,)), ((), ())), preferred_element_type=jnp.float32
    )


def rms_scale(values):
    return lax.rsqrt(jnp.mean(values * values, axis=1, keepdims=True) + EPS)


def rope_tables(position, head_size):
    half_size = head_size // 2
    inverse = jnp.exp(
        jnp.arange(half_size, dtype=jnp.float32) * (-2.0 * math.log(THETA) / head_size)
    )
    angles = position.astype(jnp.float32)[:, None] * inverse[None, :]
    return (jnp.cos(angles), jnp.sin(angles))


def apply_rotation(values, cosine_table, sine_table, head_count):
    pieces = values.reshape(values.shape[0], head_count, -1)
    half_size = pieces.shape[2] // 2
    first_half = pieces[:, :, :half_size]
    second_half = pieces[:, :, half_size:]
    cos_wide = cosine_table[:, None, :]
    sin_wide = sine_table[:, None, :]
    turned = jnp.concatenate(
        [
            first_half * cos_wide - second_half * sin_wide,
            second_half * cos_wide + first_half * sin_wide,
        ],
        axis=2,
    )
    return turned.reshape(values.shape)


def reverse_rotation(values, cosine_table, sine_table, head_count):
    pieces = values.reshape(values.shape[0], head_count, -1)
    half_size = pieces.shape[2] // 2
    first_half = pieces[:, :, :half_size]
    second_half = pieces[:, :, half_size:]
    cos_wide = cosine_table[:, None, :]
    sin_wide = sine_table[:, None, :]
    turned = jnp.concatenate(
        [
            first_half * cos_wide + second_half * sin_wide,
            second_half * cos_wide - first_half * sin_wide,
        ],
        axis=2,
    )
    return turned.reshape(values.shape)


def gather_rows(values):
    return lax.all_gather(values, "col", axis=0, tiled=True)


def regroup_tokens(values):
    return lax.all_to_all(values, "col", split_axis=0, concat_axis=1, tiled=True)


def regroup_columns(values):
    return lax.all_to_all(values, "col", split_axis=1, concat_axis=0, tiled=True)


def spread_sum(products, own_rows):
    result = jnp.zeros((lax.axis_size("col") * own_rows, products[0][1].shape[0]), jnp.float32)
    for left_mat, right_mat in products:
        result = result + matmul_nt(left_mat, right_mat)
    return lax.psum_scatter(result, "col", scatter_dimension=0, tiled=True)


def attend(query_heads, heads_of_key, heads_of_value, allowed, factor):
    heads_per_group = query_heads.shape[0] // heads_of_key.shape[0]

    def one_head(unused, element):
        query_rows, head_index = element
        key_rows = lax.dynamic_index_in_dim(
            heads_of_key, head_index // heads_per_group, 0, keepdims=False
        )
        value_rows = lax.dynamic_index_in_dim(
            heads_of_value, head_index // heads_per_group, 0, keepdims=False
        )
        scores = jnp.where(allowed, matmul_nt(query_rows, key_rows) * factor, NEG_FILL)
        row_max = jnp.max(scores, axis=1, keepdims=True)
        weights = jnp.exp(scores - row_max)
        row_total = jnp.sum(weights, axis=1, keepdims=True)
        prob_low = (weights / row_total).astype(jnp.bfloat16)
        logsum = row_max[:, 0] + jnp.log(row_total[:, 0])
        return (unused, (matmul(prob_low, value_rows), logsum))

    head_ids = jnp.arange(query_heads.shape[0], dtype=jnp.int32)
    ignored, (head_outputs, logsum) = lax.scan(
        one_head, jnp.zeros((), jnp.float32), (query_heads, head_ids)
    )
    return (head_outputs, logsum)


def attend_back(query_heads, heads_of_key, heads_of_value, grad_heads, logsum, allowed, factor):
    heads_per_group = query_heads.shape[0] // heads_of_key.shape[0]

    def one_head(state, element):
        key_acc, value_acc = state
        query_rows, grad_rows, head_sum, head_index = element
        kv_index = head_index // heads_per_group
        key_rows = lax.dynamic_index_in_dim(heads_of_key, kv_index, 0, keepdims=False)
        value_rows = lax.dynamic_index_in_dim(heads_of_value, kv_index, 0, keepdims=False)
        scores = jnp.where(allowed, matmul_nt(query_rows, key_rows) * factor, NEG_FILL)
        probs = jnp.exp(scores - head_sum[:, None])
        prob_grad = matmul_nt(grad_rows, value_rows)
        score_grad = (
            probs * (prob_grad - jnp.sum(probs * prob_grad, axis=1, keepdims=True))
        ).astype(jnp.bfloat16)
        query_grad = matmul(score_grad, key_rows) * factor
        key_grad = matmul_tn(score_grad, query_rows) * factor
        value_grad = matmul_tn(probs.astype(jnp.bfloat16), grad_rows)
        key_acc = lax.dynamic_update_index_in_dim(
            key_acc,
            lax.dynamic_index_in_dim(key_acc, kv_index, 0, keepdims=False) + key_grad,
            kv_index,
            0,
        )
        value_acc = lax.dynamic_update_index_in_dim(
            value_acc,
            lax.dynamic_index_in_dim(value_acc, kv_index, 0, keepdims=False) + value_grad,
            kv_index,
            0,
        )
        return ((key_acc, value_acc), query_grad)

    head_ids = jnp.arange(query_heads.shape[0], dtype=jnp.int32)
    empty = jnp.zeros(heads_of_key.shape, jnp.float32)
    (key_acc, value_acc), query_grads = lax.scan(
        one_head, (empty, empty), (query_heads, grad_heads, logsum, head_ids)
    )
    return (query_grads, key_acc, value_acc)


def on_device(
    layer_input,
    norm1_gain,
    w_qkv,
    w_out,
    norm2_gain,
    w_gate,
    w_up,
    w_down,
    out_cotangent,
    seq_lengths,
    position_ids,
    deal_rows,
):
    own_rows, model_width = layer_input.shape
    row_devices = lax.axis_size("row")
    col_devices = lax.axis_size("col")
    block_rows = own_rows // row_devices
    rows_per_group = own_rows * col_devices
    row_ids = jnp.arange(row_devices, dtype=jnp.int32)
    targets = deal_rows[0]
    sender = jnp.sum(jnp.where(targets[:, None] == row_ids[None, :], row_ids[:, None], 0), axis=0)
    input_blocks = jnp.take(
        layer_input.reshape(row_devices, block_rows, model_width), sender, axis=0
    ).reshape(own_rows, model_width)
    cot_blocks = jnp.take(
        out_cotangent.reshape(row_devices, block_rows, model_width), sender, axis=0
    ).reshape(own_rows, model_width)
    dealt_input, dealt_cot = (
        lax.all_to_all(input_blocks, "row", split_axis=0, concat_axis=0, tiled=True),
        lax.all_to_all(cot_blocks, "row", split_axis=0, concat_axis=0, tiled=True),
    )
    qkv_mat, out_mat, gate_mat, up_mat, down_mat = (
        lax.all_gather(w_qkv, "row", axis=0, tiled=True),
        lax.all_gather(w_out, "row", axis=0, tiled=True),
        lax.all_gather(w_gate, "row", axis=0, tiled=True),
        lax.all_gather(w_up, "row", axis=0, tiled=True),
        lax.all_gather(w_down, "row", axis=0, tiled=True),
    )
    inputs_f = dealt_input.astype(jnp.float32)
    scale_one = rms_scale(inputs_f)
    normed_one = inputs_f * scale_one
    xn_one = (normed_one * norm1_gain).astype(jnp.bfloat16)
    xn_one_rows = gather_rows(xn_one)
    query_key_value_local = regroup_tokens(matmul(xn_one_rows, qkv_mat).astype(jnp.bfloat16))
    factor = 1.0 / math.sqrt(HEAD_DIMENSION)
    cosine_table, sine_table = rope_tables(position_ids, HEAD_DIMENSION)
    query_r = apply_rotation(
        query_key_value_local[:, :QUERY_FEATURES].astype(jnp.float32),
        cosine_table,
        sine_table,
        QUERY_HEADS,
    ).astype(jnp.bfloat16)
    key_repeated = apply_rotation(
        query_key_value_local[:, QUERY_FEATURES : QUERY_FEATURES + KEY_FEATURES].astype(
            jnp.float32
        ),
        cosine_table,
        sine_table,
        KEY_VALUE_HEADS,
    ).astype(jnp.bfloat16)
    value_own = query_key_value_local[:, QUERY_FEATURES + KEY_FEATURES :]
    key_full, value_full = (
        lax.all_gather(key_repeated, "col", axis=0, tiled=True),
        lax.all_gather(value_own, "col", axis=0, tiled=True),
    )
    col_index = lax.axis_index("col")
    key_ids = jnp.arange(rows_per_group, dtype=jnp.int32)
    query_ids = col_index * own_rows + jnp.arange(own_rows, dtype=jnp.int32)
    bounds = jnp.cumsum(seq_lengths[0])
    key_seg = jnp.sum((key_ids[:, None] >= bounds[None, :]).astype(jnp.int32), axis=1)
    query_seg = jnp.sum((query_ids[:, None] >= bounds[None, :]).astype(jnp.int32), axis=1)
    allowed = (query_seg[:, None] == key_seg[None, :]) & (key_ids[None, :] <= query_ids[:, None])
    query_heads = query_r.reshape(own_rows, QUERY_HEADS, HEAD_DIMENSION).transpose(1, 0, 2)
    heads_of_key = key_full.reshape(rows_per_group, KEY_VALUE_HEADS, HEAD_DIMENSION).transpose(
        1, 0, 2
    )
    heads_of_value = value_full.reshape(rows_per_group, KEY_VALUE_HEADS, HEAD_DIMENSION).transpose(
        1, 0, 2
    )
    head_outputs, logsum = attend(query_heads, heads_of_key, heads_of_value, allowed, factor)
    attn_own = (
        head_outputs.transpose(1, 0, 2).reshape(own_rows, QUERY_FEATURES).astype(jnp.bfloat16)
    )
    attn_cols = regroup_columns(attn_own)
    attn_proj = spread_sum(((attn_cols, out_mat),), own_rows)
    residual = inputs_f + attn_proj
    scale_two = rms_scale(residual)
    normed_two = residual * scale_two
    xn_two = (normed_two * norm2_gain).astype(jnp.bfloat16)
    xn_two_rows = gather_rows(xn_two)
    gate_pre = matmul(xn_two_rows, gate_mat)
    up_pre = matmul(xn_two_rows, up_mat)
    sigmoid_gate = jax.nn.sigmoid(gate_pre)
    hidden = (gate_pre * sigmoid_gate * up_pre).astype(jnp.bfloat16)
    mlp_proj = spread_sum(((hidden, down_mat),), own_rows)
    layer_out = (residual + mlp_proj).astype(jnp.bfloat16)
    cot_f = dealt_cot.astype(jnp.float32)
    cot_rows = gather_rows(dealt_cot)
    hidden_grad = matmul(cot_rows, down_mat)
    grad_down_part = matmul_tn(cot_rows, hidden)
    gate_grad = (
        hidden_grad * up_pre * sigmoid_gate * (1.0 + gate_pre * (1.0 - sigmoid_gate))
    ).astype(jnp.bfloat16)
    up_grad = (hidden_grad * gate_pre * sigmoid_gate).astype(jnp.bfloat16)
    xn_two_grad = spread_sum(((gate_grad, gate_mat), (up_grad, up_mat)), own_rows)
    grad_gate_part = matmul_tn(xn_two_rows, gate_grad)
    grad_up_part = matmul_tn(xn_two_rows, up_grad)
    gain_two_part = jnp.sum(xn_two_grad * normed_two, axis=0)
    normed_grad = xn_two_grad * norm2_gain
    residual_grad = cot_f + scale_two * (
        normed_grad - normed_two * jnp.mean(normed_grad * normed_two, axis=1, keepdims=True)
    )
    branch_grad = residual_grad.astype(jnp.bfloat16)
    branch_rows = gather_rows(branch_grad)
    attn_grad = regroup_tokens(matmul(branch_rows, out_mat).astype(jnp.bfloat16))
    grad_out_part = matmul_tn(branch_rows, attn_cols)
    grad_heads = attn_grad.reshape(own_rows, QUERY_HEADS, HEAD_DIMENSION).transpose(1, 0, 2)
    query_grads, key_acc, value_acc = attend_back(
        query_heads, heads_of_key, heads_of_value, grad_heads, logsum, allowed, factor
    )
    key_part = key_acc.transpose(1, 0, 2).reshape(rows_per_group, KEY_FEATURES)
    value_part = value_acc.transpose(1, 0, 2).reshape(rows_per_group, KEY_FEATURES)
    key_backward, value_back = (
        lax.psum_scatter(
            key_part.astype(jnp.bfloat16), "col", scatter_dimension=0, tiled=True
        ).astype(jnp.float32),
        lax.psum_scatter(
            value_part.astype(jnp.bfloat16), "col", scatter_dimension=0, tiled=True
        ).astype(jnp.float32),
    )
    query_back = reverse_rotation(
        query_grads.transpose(1, 0, 2).reshape(own_rows, QUERY_FEATURES),
        cosine_table,
        sine_table,
        QUERY_HEADS,
    )
    key_rotated = reverse_rotation(key_backward, cosine_table, sine_table, KEY_VALUE_HEADS)
    qkv_grad = jnp.concatenate([query_back, key_rotated, value_back], axis=1).astype(jnp.bfloat16)
    qkv_cols = regroup_columns(qkv_grad)
    xn_one_grad = spread_sum(((qkv_cols, qkv_mat),), own_rows)
    grad_qkv_part = matmul_tn(xn_one_rows, qkv_cols)
    gain_one_part = jnp.sum(xn_one_grad * normed_one, axis=0)
    normed_grad_one = xn_one_grad * norm1_gain
    input_grad = residual_grad + scale_one * (
        normed_grad_one - normed_one * jnp.mean(normed_grad_one * normed_one, axis=1, keepdims=True)
    )
    grad_qkv, grad_out, grad_gate, grad_up, grad_down = (
        lax.psum_scatter(grad_qkv_part, "row", scatter_dimension=0, tiled=True),
        lax.psum_scatter(grad_out_part, "row", scatter_dimension=0, tiled=True),
        lax.psum_scatter(grad_gate_part, "row", scatter_dimension=0, tiled=True),
        lax.psum_scatter(grad_up_part, "row", scatter_dimension=0, tiled=True),
        lax.psum_scatter(grad_down_part, "row", scatter_dimension=0, tiled=True),
    )
    grad_norm1, grad_norm2 = lax.psum((gain_one_part, gain_two_part), ("row", "col"))
    back_out, back_grad = (
        lax.all_to_all(layer_out, "row", split_axis=0, concat_axis=0, tiled=True),
        lax.all_to_all(
            input_grad.astype(jnp.bfloat16), "row", split_axis=0, concat_axis=0, tiled=True
        ),
    )
    layer_output = jnp.take(
        back_out.reshape(row_devices, block_rows, model_width), targets, axis=0
    ).reshape(own_rows, model_width)
    grad_input = jnp.take(
        back_grad.reshape(row_devices, block_rows, model_width), targets, axis=0
    ).reshape(own_rows, model_width)
    return (
        layer_output,
        grad_input,
        grad_norm1,
        grad_qkv,
        grad_out,
        grad_norm2,
        grad_gate,
        grad_up,
        grad_down,
    )


def solution(mesh):
    placed = (
        P(("row", "col"), None),
        P(),
        P("row", "col"),
        P("row", "col"),
        P(),
        P("row", "col"),
        P("row", "col"),
        P("row", "col"),
        P(("row", "col"), None),
        P("row", None),
        P(("row", "col")),
        P(("row", "col"), None),
    )
    return jax.shard_map(
        on_device,
        mesh=mesh,
        in_specs=placed,
        out_specs=(
            P(("row", "col"), None),
            P(("row", "col"), None),
            P(),
            P("row", "col"),
            P("row", "col"),
            P(),
            P("row", "col"),
            P("row", "col"),
            P("row", "col"),
        ),
        check_vma=False,
    )
```

profile of v0, /device:TPU:0, one launch (start us, length us, event | category | flops | bytes accessed | tf_op | source)
XLA Modules:
  0.0 1575.9 jit_solution(9520040302750912809)
XLA Ops:
  13.4 32.9 %all_to_all.100 = bf16[8,64,960]{2,1,0:T(8,128)(2,1)S(1)} all-to-all(bf16[8,64,960]{2,1,0:T(8,128)(2,1)S(1)} %get-tuple-element.545), channel_id=1, replica_groups=mesh['row'=8,'col'=4] {'row'}, dimensions={0} | all-to-all | bytes 1966080 | tf_op jit(solution)/shard_map/all_to_all | solution.py:194
  48.7 32.4 %all-gather = bf16[8,120,400]{1,2,0:T(8,128)(2,1)S(1)} all-gather(bf16[1,120,400]{1,2,0:T(8,128)(2,1)S(1)} %bitcast.267), channel_id=1, replica_groups=mesh['row'=8,'col'=4] {'row'}, dimensions={0}, use_global_device_ids=true | all-gather | bytes 864000 | tf_op jit(solution)/shard_map/all_gather | solution.py:198
  82.8 4.2 convolution_convert_fusion
  88.4 4.4 all-to-all-start.1
  93.2 20.4 %all-to-all-done.1 = bf16[4,512,400]{1,2,0:T(8,128)(2,1)} async-done(((bf16[4,512,400]{1,2,0:T(8,128)(2,1)}), bf16[4,512,400]{1,2,0:T(8,128)(2,1)}, u32[]{:S(2)}, u32[]{:S(2)}) %all-to-all-start.1) | async-done | bytes 1638432 | tf_op jit(solution)/shard_map/all_to_all | solution.py:85
  122.2 10.6 all-gather.13.cloned.1.call-done
  132.8 3.8 copy.90
  136.6 16.6 %all-gather.15.cloned.1.call-done = bf16[2048,320]{0,1:T(8,128)(2,1)} async-done(((bf16[512,320]{0,1:T(8,128)(2,1)}), bf16[2048,320]{0,1:T(8,128)(2,1)}) %all-gather.15.cloned.1.call-update) | async-done | bytes 1310736 | tf_op jit(solution)/shard_map/all_gather | solution.py:229
  153.1 3.8 copy.91
  156.9 146.1 %while.34 = (s32[]{:T(128)}, bf16[15,512,64]{1,2,0:T(8,128)(2,1)}, f32[15,512]{1,0:T(8,128)}, bf16[15,512,64]{2,1,0:T(8,128)(2,1)}, s32[15]{0:T(128)S(1)}, /*ind...) while((s32[]{:T(128)}, bf16[15,512,64]{1,2,0:T(8,128)(2,1)}, ...), condition=%wide.region_8.10_spmd.clone.clone, body=%wide.region_5.9_spmd.clone.sunk.clone | while | flops 279969280 | bytes 13926677 | solution.py:119
  303.0 3.5 all-to-all-start.2
  306.6 31.5 %all_gather.37 = bf16[960,240]{1,0:T(8,128)(2,1)S(1)} all-gather(bf16[120,240]{1,0:T(8,128)(2,1)S(1)} %copy-done.24), channel_id=1, replica_groups=mesh['row'=8,'col'=4] {'row'}, dimensions={0}, use_global_device_ids=true | all-gather | bytes 518400 | tf_op jit(solution)/shard_map/all_gather | solution.py:199
  339.1 4.3 fusion.59
  344.3 69.5 %reduce-scatter.20.cloned.1.call-done = f32[512,960]{0,1:T(8,128)} async-done(((f32[2048,960]{0,1:T(8,128)}), f32[512,960]{0,1:T(8,128)}) %reduce-scatter.20.cloned.1.call-update) | async-done | bytes 1966096 | tf_op jit(solution)/shard_map/reduce_scatter | solution.py:96
  419.7 31.2 %all_to_all.101 = bf16[8,64,960]{2,1,0:T(8,128)(2,1)} all-to-all(bf16[8,64,960]{2,1,0:T(8,128)(2,1)S(1)} %copy-done.8), channel_id=1, replica_groups=mesh['row'=8,'col'=4] {'row'}, dimensions={0} | all-to-all | bytes 1966080 | tf_op jit(solution)/shard_map/all_to_all | solution.py:195
  451.3 8.3 fusion.50
  459.6 35.7 %all-gather.19.cloned.1.call-done = bf16[960,640]{1,0:T(8,128)(2,1)} async-done(((bf16[120,640]{1,0:T(8,128)(2,1)}), bf16[960,640]{1,0:T(8,128)(2,1)}) %all-gather.19.cloned.1.call-update) | async-done | bytes 1228816 | tf_op jit(solution)/shard_map/all_gather | solution.py:200
  495.3 8.3 fusion.49
  503.6 34.6 %all-gather.23.cloned.1.call-done = bf16[960,640]{1,0:T(8,128)(2,1)} async-done(((bf16[120,640]{1,0:T(8,128)(2,1)}), bf16[960,640]{1,0:T(8,128)(2,1)}) %all-gather.23.cloned.1.call-update) | async-done | bytes 1228816 | tf_op jit(solution)/shard_map/all_gather | solution.py:202
  538.2 34.7 %all-gather.25.cloned.1.call-done = bf16[2048,960]{1,0:T(8,128)(2,1)} async-done(((bf16[512,960]{1,0:T(8,128)(2,1)}), bf16[2048,960]{1,0:T(8,128)(2,1)}) %all-gather.25.cloned.1.call-update) | async-done | bytes 3932176 | tf_op jit(solution)/shard_map/all_gather | solution.py:81
  572.9 10.5 multiply_convert_fusion.1
  586.7 5.4 convolution_add_fusion.1
  594.6 66.5 %reduce-scatter.24.cloned.1.call-done = f32[512,960]{0,1:T(8,128)} async-done(((f32[2048,960]{0,1:T(8,128)}), f32[512,960]{0,1:T(8,128)}) %reduce-scatter.24.cloned.1.call-update) | async-done | bytes 1966096 | tf_op jit(solution)/shard_map/reduce_scatter | solution.py:96
  664.9 33.2 %all-gather.27.cloned.1.call-done = bf16[2048,960]{0,1:T(8,128)(2,1)} async-done(((bf16[512,960]{0,1:T(8,128)(2,1)}), bf16[2048,960]{0,1:T(8,128)(2,1)}) %all-gather.27.cloned.1.call-update) | async-done | bytes 3932176 | tf_op jit(solution)/shard_map/all_gather | solution.py:81
  706.0 13.7 all-to-all-done.5
  722.7 236.6 %while.35 = (s32[]{:T(128)}, f32[5,2048,64]{1,2,0:T(8,128)}, f32[5,2048,64]{1,2,0:T(8,128)S(1)}, f32[15,512,64]{1,2,0:T(8,128)}, s32[15]{0:T(128)S(1)}, /*index=...) while((s32[]{:T(128)}, f32[5,2048,64]{1,2,0:T(8,128)}, ...), condition=%wide.region_16.18_spmd.clone.clone, body=%wide.region_14.17_spmd.clone.sunk.clone | while | flops 684097024 | bytes 37771592 | solution.py:159
  965.7 23.3 %reduce-scatter.26.cloned.1.call-done = bf16[512,320]{0,1:T(8,128)(2,1)} async-done(((bf16[2048,320]{0,1:T(8,128)(2,1)}), bf16[512,320]{0,1:T(8,128)(2,1)}) %reduce-scatter.26.cloned.1.call-update) | async-done | bytes 327696 | tf_op jit(solution)/shard_map/reduce_scatter | solution.py:289
  990.2 28.1 %reduce-scatter.28.cloned.1.call-done = bf16[512,320]{0,1:T(8,128)(2,1)} async-done(((bf16[2048,320]{0,1:T(8,128)(2,1)}), bf16[512,320]{0,1:T(8,128)(2,1)}) %reduce-scatter.28.cloned.1.call-update) | async-done | bytes 327696 | tf_op jit(solution)/shard_map/reduce_scatter | solution.py:292
  1019.4 23.3 %all_to_all.102 = bf16[512,4,400]{0,2,1:T(8,128)(2,1)S(1)} all-to-all(bf16[512,4,400]{0,2,1:T(8,128)(2,1)S(1)} %bitcast.241), channel_id=1, replica_groups=mesh['row'=8,'col'=4] {'col'}, dimensions={1} | all-to-all | bytes 3276800 | tf_op jit(solution)/shard_map/all_to_all | solution.py:89
  1043.0 5.3 fusion.53
  1049.6 7.9 fusion.51
  1057.6 6.5 fusion.54
  1064.4 7.9 fusion.58
  1072.4 7.9 fusion.56
  1080.4 6.8 fusion.57
  1087.2 30.1 %reduce-scatter.30.cloned.1.call-done = f32[512,960]{0,1:T(8,128)} async-done(((f32[2048,960]{0,1:T(8,128)}), f32[512,960]{0,1:T(8,128)}) %reduce-scatter.30.cloned.1.call-update) | async-done | bytes 1966096 | tf_op jit(solution)/shard_map/reduce_scatter | solution.py:96
  1119.5 69.3 %reduce-scatter.22.cloned.1.call-done = f32[512,960]{0,1:T(8,128)} async-done(((f32[2048,960]{0,1:T(8,128)}), f32[512,960]{0,1:T(8,128)}) %reduce-scatter.22.cloned.1.call-update) | async-done | bytes 1966096 | tf_op jit(solution)/shard_map/reduce_scatter | solution.py:96
  1188.8 4.7 add_convert_fusion
  1195.9 5.6 all-to-all-start.7
  1202.9 38.0 %all-to-all-done.7 = bf16[8,64,960]{2,1,0:T(8,128)(2,1)S(1)} async-done(((bf16[8,64,960]{2,1,0:T(8,128)(2,1)}), bf16[8,64,960]{2,1,0:T(8,128)(2,1)S(1)}, u32[]{:S(2)}, u32[]{:S(2)}) %all-to-all-start.7) | async-done | bytes 983072 | tf_op jit(solution)/shard_map/all_to_all | solution.py:322
  1240.8 3.6 all-to-all-start.3
  1244.5 4.4 fusion.55
  1248.9 31.4 %reduce-scatter.34.cloned.1.call-done = f32[120,400]{1,0:T(8,128)} async-done(((f32[960,400]{1,0:T(8,128)}), f32[120,400]{1,0:T(8,128)}) %reduce-scatter.34.cloned.1.call-update) | async-done | bytes 192016
  1282.1 39.7 %all-reduce.3 = (f32[960]{0:T(1024)}, f32[960]{0:T(1024)}) all-reduce(f32[960]{0:T(1024)S(1)} %get-tuple-element.467, f32[960]{0:T(1024)S(1)} %get-tuple-element.465), channel_id=1, replica_groups=mesh['row'=8,'col'=4] {'row','col'}, use_global_device_ids=true, to_apply=%region_22.24 | all-reduce | flops 1920 | bytes 15360 | tf_op jit(solution)/shard_map/psum | solution.py:319
  1327.9 26.9 %reduce-scatter.40.cloned.1.call-done = f32[120,640]{1,0:T(8,128)} async-done(((f32[960,640]{1,0:T(8,128)}), f32[120,640]{1,0:T(8,128)}) %reduce-scatter.40.cloned.1.call-update) | async-done | bytes 307216
  1354.8 73.3 %reduce-scatter.36.cloned.1.call-done = f32[120,640]{1,0:T(8,128)} async-done(((f32[960,640]{1,0:T(8,128)}), f32[120,640]{1,0:T(8,128)}) %reduce-scatter.36.cloned.1.call-update) | async-done | bytes 307216
  1428.1 73.4 %reduce-scatter.38.cloned.1.call-done = f32[120,640]{1,0:T(8,128)} async-done(((f32[960,640]{1,0:T(8,128)}), f32[120,640]{1,0:T(8,128)}) %reduce-scatter.38.cloned.1.call-update) | async-done | bytes 307216
  1501.5 66.6 %reduce-scatter.32.cloned.1.call-done = f32[120,240]{1,0:T(8,128)} async-done(((f32[960,240]{1,0:T(8,128)}), f32[120,240]{1,0:T(8,128)}) %reduce-scatter.32.cloned.1.call-update) | async-done | bytes 115216 | tf_op jit(solution)/shard_map/reduce_scatter | solution.py:314
  (414 shorter events, 395.2 us)
Async XLA Ops:
  8.0 74.8 %all-gather.11.cloned.1.call-start = ((), (), s32[]{:S(2)}) async-start(), calls=%async_computation.19 | async-start | bytes 4915200 | tf_op jit(solution)/shard_map/all_gather | solution.py:81
  13.4 33.8 %copy-start.25 = (f32[960]{0:T(1024)S(1)}, f32[960]{0:T(1024)}, u32[]{:S(2)}) copy-start(f32[960]{0:T(1024)} %param.19) | copy-start | bytes 11524
  47.3 366.5 %copy-start = (f32[512,960]{0,1:T(8,128)}, f32[512,960]{0,1:T(8,128)S(1)}, u32[]{:S(2)}) copy-start(f32[512,960]{0,1:T(8,128)S(1)} %copy.93) | copy-start | bytes 5898244
  87.0 5.8 copy-start.29
  88.4 25.2 %all-to-all-start.1 = ((bf16[4,512,400]{1,2,0:T(8,128)(2,1)}), bf16[4,512,400]{1,2,0:T(8,128)(2,1)}, u32[]{:S(2)}, u32[]{:S(2)}) async-start(bf16[4,512,400]{1,2,0:T(8,128)(2,1)} %bitcast.240), calls=%async_computation.1 | async-start | bytes 3276800 | tf_op jit(solution)/shard_map/all_to_all | solution.py:85
  92.7 24.4 %copy-start.32 = (s32[1,3]{1,0:T(1,128)S(1)}, s32[1,3]{1,0:T(1,128)}, u32[]{:S(2)}) copy-start(s32[1,3]{1,0:T(1,128)} %param.27) | copy-start | bytes 40
  92.7 40.0 %all-gather.13.cloned.1.call-start = ((), (), s32[]{:S(2)}) async-start(), calls=%async_computation.20 | async-start | bytes 1638400 | tf_op jit(solution)/shard_map/all_gather | solution.py:228
  93.1 26.9 %copy-start.15 = (f32[512,32]{0,1:T(8,128)}, f32[512,32]{0,1:T(8,128)S(1)}, u32[]{:S(2)}) copy-start(f32[512,32]{0,1:T(8,128)S(1)} %get-tuple-element.540) | copy-start | bytes 196612
  93.2 26.9 %copy-start.17 = (f32[512,32]{0,1:T(8,128)}, f32[512,32]{0,1:T(8,128)S(1)}, u32[]{:S(2)}) copy-start(f32[512,32]{0,1:T(8,128)S(1)} %get-tuple-element.541) | copy-start | bytes 196612
  116.4 36.8 %all-gather.15.cloned.1.call-start = ((), (), s32[]{:S(2)}) async-start(), calls=%async_computation.21 | async-start | bytes 1638400 | tf_op jit(solution)/shard_map/all_gather | solution.py:229
  156.9 149.7 %copy-start.24 = (bf16[120,240]{1,0:T(8,128)(2,1)S(1)}, bf16[120,240]{1,0:T(8,128)(2,1)}, u32[]{:S(2)}) copy-start(bf16[120,240]{1,0:T(8,128)(2,1)} %param.21) | copy-start | bytes 172804
  303.0 35.1 %all-to-all-start.2 = ((bf16[512,4,240]{0,2,1:T(8,128)(2,1)}), bf16[512,4,240]{0,2,1:T(8,128)(2,1)S(1)}, u32[]{:S(2)}, u32[]{:S(2)}) async-start(bf16[512,4,240]{0,2,1:T(8,128)(2,1)} %bitcast.20), calls=%async_computation.2 | async-start | bytes 1966080 | tf_op jit(solution)/shard_map/all_to_all | solution.py:89
  306.5 107.3 %reduce-scatter.20.cloned.1.call-start = ((), (), s32[]{:S(2)}) async-start(), calls=%async_computation.22 | async-start | bytes 9830400 | tf_op jit(solution)/shard_map/reduce_scatter | solution.py:96
  343.4 107.5 %all-gather.21.cloned.1.call-start = ((), (), s32[]{:S(2)}) async-start(), calls=%async_computation.25 | async-start | bytes 1382400 | tf_op jit(solution)/shard_map/all_gather | solution.py:201
  344.0 73.1 %copy-start.23 = (f32[960]{0:T(1024)S(1)}, f32[960]{0:T(1024)}, u32[]{:S(2)}) copy-start(f32[960]{0:T(1024)} %param.22) | copy-start | bytes 11524
  344.0 107.2 %all-gather.17.cloned.1.call-start = ((), (), s32[]{:S(2)}) async-start(), calls=%async_computation.23 | async-start | bytes 4915200 | tf_op jit(solution)/shard_map/all_gather | solution.py:81
  415.8 4.0 copy-start.8
  418.3 76.9 %all-gather.19.cloned.1.call-start = ((), (), s32[]{:S(2)}) async-start(), calls=%async_computation.24 | async-start | bytes 1382400 | tf_op jit(solution)/shard_map/all_gather | solution.py:200
  418.9 119.2 %all-gather.23.cloned.1.call-start = ((), (), s32[]{:S(2)}) async-start(), calls=%async_computation.26 | async-start | bytes 1382400 | tf_op jit(solution)/shard_map/all_gather | solution.py:202
  419.7 153.2 %all-gather.25.cloned.1.call-start = ((), (), s32[]{:S(2)}) async-start(), calls=%async_computation.28 | async-start | bytes 5242880 | tf_op jit(solution)/shard_map/all_gather | solution.py:81
  450.9 210.2 %reduce-scatter.24.cloned.1.call-start = ((), (), s32[]{:S(2)}) async-start(), calls=%async_computation.29 | async-start | bytes 9830400 | tf_op jit(solution)/shard_map/reduce_scatter | solution.py:96
  503.6 79.8 %copy-start.31 = (bf16[960,640]{1,0:T(8,128)(2,1)S(1)}, bf16[960,640]{1,0:T(8,128)(2,1)}, u32[]{:S(2)}) copy-start(bf16[960,640]{1,0:T(8,128)(2,1)} %all-gather.19.cloned.1.call-done) | copy-start | bytes 3686404
  583.4 3.3 copy-start.9
  583.4 3.3 copy-start.19
  592.1 69.0 %copy-start.3 = (f32[512,960]{0,1:T(8,128)S(1)}, f32[512,960]{0,1:T(8,128)}, u32[]{:S(2)}) copy-start(f32[512,960]{0,1:T(8,128)} %copy-done.2) | copy-start | bytes 5898244
  592.1 106.0 %all-gather.27.cloned.1.call-start = ((), (), s32[]{:S(2)}) async-start(), calls=%async_computation.30 | async-start | bytes 4915200 | tf_op jit(solution)/shard_map/all_gather | solution.py:81
  594.6 68.8 %copy-start.6 = (bf16[512,960]{0,1:T(8,128)(2,1)S(1)}, bf16[512,960]{0,1:T(8,128)(2,1)}, u32[]{:S(2)}) copy-start(bf16[512,960]{0,1:T(8,128)(2,1)} %copy.96) | copy-start | bytes 2949124
  702.4 17.2 %all-to-all-start.5 = ((bf16[4,512,240]{1,2,0:T(8,128)(2,1)}), bf16[4,512,240]{1,2,0:T(8,128)(2,1)S(1)}, u32[]{:S(2)}, u32[]{:S(2)}) async-start(bf16[4,512,240]{1,2,0:T(8,128)(2,1)} %bitcast.164), calls=%async_computation.8 | async-start | bytes 1966080 | tf_op jit(solution)/shard_map/all_to_all | solution.py:85
  705.9 283.1 %reduce-scatter.26.cloned.1.call-start = ((), (), s32[]{:S(2)}) async-start(), calls=%async_computation.31 | async-start | bytes 1638400 | tf_op jit(solution)/shard_map/reduce_scatter | solution.py:289
  962.3 56.0 %reduce-scatter.28.cloned.1.call-start = ((), (), s32[]{:S(2)}) async-start(), calls=%async_computation.32 | async-start | bytes 1638400 | tf_op jit(solution)/shard_map/reduce_scatter | solution.py:292
  963.7 153.6 %reduce-scatter.30.cloned.1.call-start = ((), (), s32[]{:S(2)}) async-start(), calls=%async_computation.33 | async-start | bytes 9830400 | tf_op jit(solution)/shard_map/reduce_scatter | solution.py:96
  1019.4 23.6 %copy-start.21 = (bf16[960,400]{0,1:T(8,128)(2,1)S(1)}, bf16[960,400]{0,1:T(8,128)(2,1)}, u32[]{:S(2)}) copy-start(bf16[960,400]{0,1:T(8,128)(2,1)} %reshape.338) | copy-start | bytes 2304004
  1048.4 140.5 %reduce-scatter.22.cloned.1.call-start = ((), (), s32[]{:S(2)}) async-start(), calls=%async_computation.27 | async-start | bytes 9830400 | tf_op jit(solution)/shard_map/reduce_scatter | solution.py:96
  1057.5 222.8 %reduce-scatter.34.cloned.1.call-start = ((), (), s32[]{:S(2)}) async-start(), calls=%async_computation.35 | async-start | bytes 2211840
  1064.2 290.7 %reduce-scatter.40.cloned.1.call-start = ((), (), s32[]{:S(2)}) async-start(), calls=%async_computation.38 | async-start | bytes 2764800
  1072.3 8.1 copy-start.10
  1072.3 355.8 %reduce-scatter.36.cloned.1.call-start = ((), (), s32[]{:S(2)}) async-start(), calls=%async_computation.36 | async-start | bytes 2764800
  1080.3 37.0 %copy-start.26 = (f32[960]{0:T(1024)S(1)}, f32[960]{0:T(1024)}, u32[]{:S(2)}) copy-start(f32[960]{0:T(1024)} %param.19) | copy-start | bytes 11524
  1080.4 37.0 %copy-start.28 = (f32[512]{0:T(512)S(1)}, f32[512]{0:T(512)}, u32[]{:S(2)}) copy-start(f32[512]{0:T(512)} %copy-done.27) | copy-start | bytes 6148
  1080.4 421.2 %reduce-scatter.38.cloned.1.call-start = ((), (), s32[]{:S(2)}) async-start(), calls=%async_computation.37 | async-start | bytes 2764800
  1087.2 30.1 %copy-start.1 = (f32[512,960]{0,1:T(8,128)S(1)}, f32[512,960]{0,1:T(8,128)}, u32[]{:S(2)}) copy-start(f32[512,960]{0,1:T(8,128)} %copy-done) | copy-start | bytes 5898244
  1087.2 101.6 %copy-start.7 = (bf16[512,960]{0,1:T(8,128)(2,1)S(1)}, bf16[512,960]{0,1:T(8,128)(2,1)}, u32[]{:S(2)}) copy-start(bf16[512,960]{0,1:T(8,128)(2,1)} %copy.96) | copy-start | bytes 2949124
  1193.6 8.0 copy-start.13
  1195.9 48.6 %copy-start.12 = (bf16[4,30,8,512]{3,2,0,1:T(8,128)(2,1)S(1)}, bf16[4,30,8,512]{3,2,0,1:T(8,128)(2,1)}, u32[]{:S(2)}) copy-start(bf16[4,30,8,512]{3,2,0,1:T(8,128)(2,1)} %copy-done.11) | copy-start | bytes 2949124
  1195.9 44.9 %all-to-all-start.7 = ((bf16[8,64,960]{2,1,0:T(8,128)(2,1)}), bf16[8,64,960]{2,1,0:T(8,128)(2,1)S(1)}, u32[]{:S(2)}, u32[]{:S(2)}) async-start(bf16[8,64,960]{2,1,0:T(8,128)(2,1)} %bitcast.42), calls=%async_computation.13 | async-start | bytes 2097152 | tf_op jit(solution)/shard_map/all_to_all | solution.py:322
  1240.8 81.6 %all-to-all-start.3 = ((bf16[8,64,960]{2,1,0:T(8,128)(2,1)}), bf16[8,64,960]{2,1,0:T(8,128)(2,1)S(1)}, u32[]{:S(2)}, u32[]{:S(2)}) async-start(bf16[8,64,960]{2,1,0:T(8,128)(2,1)} %bitcast.22), calls=%async_computation.5 | async-start | bytes 2097152 | tf_op jit(solution)/shard_map/all_to_all | solution.py:321
  1244.4 4.5 copy-start.33
  1244.4 323.7 %reduce-scatter.32.cloned.1.call-start = ((), (), s32[]{:S(2)}) async-start(), calls=%async_computation.34 | async-start | bytes 1105920 | tf_op jit(solution)/shard_map/reduce_scatter | solution.py:314
  (12 other events, 19.8 us)
Sparse Core Ops, SparseCore 0:
  48.8 32.0 all-gather.10
  116.5 16.2 all-gather.12
  134.9 18.1 all-gather.14
  343.6 70.1 reduce-scatter.19
  665.0 32.9 all-gather.26
  962.5 26.5 reduce-scatter.25
  991.7 26.5 reduce-scatter.27
Sparse Core Ops, SparseCore 1:
  346.1 42.9 all-gather.20
  418.4 32.8 all-gather.16
  453.6 41.7 all-gather.18
  497.7 40.4 all-gather.22
  539.8 33.0 all-gather.24
  592.2 68.8 reduce-scatter.23
  1048.4 68.9 reduce-scatter.29
  1119.9 68.8 reduce-scatter.21
  1192.2 88.1 reduce-scatter.33
  1285.0 69.8 reduce-scatter.39
  1359.3 68.7 reduce-scatter.35
  1432.8 68.7 reduce-scatter.37
  1505.7 62.3 reduce-scatter.31
where the time goes:
time: 1590 us; the launch traced here: 1580 us
  waiting for transfers between devices  799 us (50%)
  matrix products  335 us (21%)
  blocking collectives  191 us (12%)
  local copies, waits for them, and re-layouts  105 us (7%)
  loops' own time  59.9 us (4%)
  other arithmetic  47.7 us (3%)
  starting transfers between devices  21.8 us (1%)
  between operations  16.8 us (1%)
    reduce_scatter x4, waiting for transfers between devices, spread_sum(): return lax.psum_scatter(result, 'col', scatter_dimension=0, tiled=True)  235 us
    unnamed x24, waiting for transfers between devices  208 us
    dot_general x50, matrix products, matmul_nt(): lax.dot_general(left_mat, right_mat, (((1,), (1,)), ((), ())), preferred_...  134 us
    dot_general x35, matrix products, matmul(): return jnp.dot(left_mat, right_mat, preferred_element_type=jnp.float32)  113 us
    dot_general x34, matrix products, matmul_tn(): lax.dot_general(left_mat, right_mat, (((0,), (0,)), ((), ())), preferred_...  80.8 us
    all_gather x4, waiting for transfers between devices, gather_rows(): return lax.all_gather(values, 'col', axis=0, tiled=True)  68.1 us
    reduce_scatter x1, waiting for transfers between devices, on_device(): lax.psum_scatter(grad_out_part, 'row', scatter_dimension=0, tiled=True)  66.6 us
    psum x1, blocking collectives, on_device(): lax.psum((gain_one_part, gain_two_part), ('row', 'col'))  39.7 us
  transfers between devices with their start and end apart: 25, of which 21 were waited for; matrix products, arithmetic and copies ran while one was open for 6% of the time, Pallas kernels for 0%

commit v1 on v0

--- a/solution.py
+++ b/solution.py
@@ -316,7 +316,7 @@
         lax.psum_scatter(grad_up_part, "row", scatter_dimension=0, tiled=True),
         lax.psum_scatter(grad_down_part, "row", scatter_dimension=0, tiled=True),
     )
-    grad_norm1, grad_norm2 = lax.psum((gain_one_part, gain_two_part), ("row", "col"))
+    grad_norm1, grad_norm2 = lax.psum(lax.psum((gain_one_part, gain_two_part), "col"), "row")
     back_out, back_grad = (
         lax.all_to_all(layer_out, "row", split_axis=0, concat_axis=0, tiled=True),
         lax.all_to_all(

time: 1590 us -> 1590 us (level)
    psum x1 -> x2, blocking collectives: 39.7 us -> 26.4 us  [the longest x1 20.7 us: on_device(): lax.psum(lax.psum((gain_one_part, gain_two_part), 'col'), 'row')]
where the time goes in v1:
time: 1590 us; the launch traced here: 1580 us
  waiting for transfers between devices  812 us (51%)
  matrix products  335 us (21%)
  blocking collectives  178 us (11%)
  local copies, waits for them, and re-layouts  105 us (7%)
  loops' own time  59.9 us (4%)
  other arithmetic  47.8 us (3%)
  starting transfers between devices  21.8 us (1%)
  between operations  16.8 us (1%)
    reduce_scatter x4, waiting for transfers between devices, spread_sum(): return lax.psum_scatter(result, 'col', scatter_dimension=0, tiled=True)  235 us
    unnamed x24, waiting for transfers between devices  221 us
    dot_general x50, matrix products, matmul_nt(): lax.dot_general(left_mat, right_mat, (((1,), (1,)), ((), ())), preferred_...  134 us
    dot_general x35, matrix products, matmul(): return jnp.dot(left_mat, right_mat, preferred_element_type=jnp.float32)  113 us
    dot_general x34, matrix products, matmul_tn(): lax.dot_general(left_mat, right_mat, (((0,), (0,)), ((), ())), preferred_...  80.8 us
    all_gather x4, waiting for transfers between devices, gather_rows(): return lax.all_gather(values, 'col', axis=0, tiled=True)  68.1 us
    reduce_scatter x1, waiting for transfers between devices, on_device(): lax.psum_scatter(grad_out_part, 'row', scatter_dimension=0, tiled=True)  66.6 us
    all_to_all x1, waiting for transfers between devices, on_device(): lax.all_to_all(input_grad.astype(jnp.bfloat16), 'row', split_axis=0, conc...  38 us
  transfers between devices with their start and end apart: 25, of which 21 were waited for; matrix products, arithmetic and copies ran while one was open for 6% of the time, Pallas kernels for 0%

profile of v1, /device:TPU:0, one launch (start us, length us, event | category | flops | bytes accessed | tf_op | source)
XLA Modules:
  0.0 1575.9 jit_solution(9671384849987366876)
XLA Ops:
  13.4 32.9 %all_to_all.100 = bf16[8,64,960]{2,1,0:T(8,128)(2,1)S(1)} all-to-all(bf16[8,64,960]{2,1,0:T(8,128)(2,1)S(1)} %get-tuple-element.547), channel_id=1, replica_groups=mesh['row'=8,'col'=4] {'row'}, dimensions={0} | all-to-all | bytes 1966080 | tf_op jit(solution)/shard_map/all_to_all | solution.py:194
  48.7 32.4 %all-gather = bf16[8,120,400]{1,2,0:T(8,128)(2,1)S(1)} all-gather(bf16[1,120,400]{1,2,0:T(8,128)(2,1)S(1)} %bitcast.267), channel_id=1, replica_groups=mesh['row'=8,'col'=4] {'row'}, dimensions={0}, use_global_device_ids=true | all-gather | bytes 864000 | tf_op jit(solution)/shard_map/all_gather | solution.py:198
  82.8 4.2 convolution_convert_fusion
  88.4 4.4 all-to-all-start.1
  93.2 20.4 %all-to-all-done.1 = bf16[4,512,400]{1,2,0:T(8,128)(2,1)} async-done(((bf16[4,512,400]{1,2,0:T(8,128)(2,1)}), bf16[4,512,400]{1,2,0:T(8,128)(2,1)}, u32[]{:S(2)}, u32[]{:S(2)}) %all-to-all-start.1) | async-done | bytes 1638432 | tf_op jit(solution)/shard_map/all_to_all | solution.py:85
  122.3 10.5 all-gather.13.cloned.1.call-done
  132.8 3.8 copy.90
  136.6 16.6 %all-gather.15.cloned.1.call-done = bf16[2048,320]{0,1:T(8,128)(2,1)} async-done(((bf16[512,320]{0,1:T(8,128)(2,1)}), bf16[2048,320]{0,1:T(8,128)(2,1)}) %all-gather.15.cloned.1.call-update) | async-done | bytes 1310736 | tf_op jit(solution)/shard_map/all_gather | solution.py:229
  153.2 3.8 copy.91
  157.0 146.1 %while.34 = (s32[]{:T(128)}, bf16[15,512,64]{1,2,0:T(8,128)(2,1)}, f32[15,512]{1,0:T(8,128)}, bf16[15,512,64]{2,1,0:T(8,128)(2,1)}, s32[15]{0:T(128)S(1)}, /*ind...) while((s32[]{:T(128)}, bf16[15,512,64]{1,2,0:T(8,128)(2,1)}, ...), condition=%wide.region_8.10_spmd.clone.clone, body=%wide.region_5.9_spmd.clone.sunk.clone | while | flops 279969280 | bytes 13926677 | solution.py:119
  306.6 31.5 %all_gather.37 = bf16[960,240]{1,0:T(8,128)(2,1)S(1)} all-gather(bf16[120,240]{1,0:T(8,128)(2,1)S(1)} %copy-done.24), channel_id=1, replica_groups=mesh['row'=8,'col'=4] {'row'}, dimensions={0}, use_global_device_ids=true | all-gather | bytes 518400 | tf_op jit(solution)/shard_map/all_gather | solution.py:199
  339.2 4.3 fusion.59
  344.3 69.5 %reduce-scatter.20.cloned.1.call-done = f32[512,960]{0,1:T(8,128)} async-done(((f32[2048,960]{0,1:T(8,128)}), f32[512,960]{0,1:T(8,128)}) %reduce-scatter.20.cloned.1.call-update) | async-done | bytes 1966096 | tf_op jit(solution)/shard_map/reduce_scatter | solution.py:96
  419.8 31.2 %all_to_all.101 = bf16[8,64,960]{2,1,0:T(8,128)(2,1)} all-to-all(bf16[8,64,960]{2,1,0:T(8,128)(2,1)S(1)} %copy-done.8), channel_id=1, replica_groups=mesh['row'=8,'col'=4] {'row'}, dimensions={0} | all-to-all | bytes 1966080 | tf_op jit(solution)/shard_map/all_to_all | solution.py:195
  451.3 8.3 fusion.50
  459.6 35.7 %all-gather.19.cloned.1.call-done = bf16[960,640]{1,0:T(8,128)(2,1)} async-done(((bf16[120,640]{1,0:T(8,128)(2,1)}), bf16[960,640]{1,0:T(8,128)(2,1)}) %all-gather.19.cloned.1.call-update) | async-done | bytes 1228816 | tf_op jit(solution)/shard_map/all_gather | solution.py:200
  495.3 8.3 fusion.49
  503.6 34.6 %all-gather.23.cloned.1.call-done = bf16[960,640]{1,0:T(8,128)(2,1)} async-done(((bf16[120,640]{1,0:T(8,128)(2,1)}), bf16[960,640]{1,0:T(8,128)(2,1)}) %all-gather.23.cloned.1.call-update) | async-done | bytes 1228816 | tf_op jit(solution)/shard_map/all_gather | solution.py:202
  538.2 34.7 %all-gather.25.cloned.1.call-done = bf16[2048,960]{1,0:T(8,128)(2,1)} async-done(((bf16[512,960]{1,0:T(8,128)(2,1)}), bf16[2048,960]{1,0:T(8,128)(2,1)}) %all-gather.25.cloned.1.call-update) | async-done | bytes 3932176 | tf_op jit(solution)/shard_map/all_gather | solution.py:81
  572.9 10.5 multiply_convert_fusion.1
  586.7 5.4 convolution_add_fusion.1
  594.6 66.5 %reduce-scatter.24.cloned.1.call-done = f32[512,960]{0,1:T(8,128)} async-done(((f32[2048,960]{0,1:T(8,128)}), f32[512,960]{0,1:T(8,128)}) %reduce-scatter.24.cloned.1.call-update) | async-done | bytes 1966096 | tf_op jit(solution)/shard_map/reduce_scatter | solution.py:96
  664.9 33.2 %all-gather.27.cloned.1.call-done = bf16[2048,960]{0,1:T(8,128)(2,1)} async-done(((bf16[512,960]{0,1:T(8,128)(2,1)}), bf16[2048,960]{0,1:T(8,128)(2,1)}) %all-gather.27.cloned.1.call-update) | async-done | bytes 3932176 | tf_op jit(solution)/shard_map/all_gather | solution.py:81
  706.0 13.7 all-to-all-done.5
  722.7 236.5 %while.35 = (s32[]{:T(128)}, f32[5,2048,64]{1,2,0:T(8,128)}, f32[5,2048,64]{1,2,0:T(8,128)S(1)}, f32[15,512,64]{1,2,0:T(8,128)}, s32[15]{0:T(128)S(1)}, /*index=...) while((s32[]{:T(128)}, f32[5,2048,64]{1,2,0:T(8,128)}, ...), condition=%wide.region_16.18_spmd.clone.clone, body=%wide.region_14.17_spmd.clone.sunk.clone | while | flops 684097024 | bytes 37771592 | solution.py:159
  965.7 23.3 %reduce-scatter.26.cloned.1.call-done = bf16[512,320]{0,1:T(8,128)(2,1)} async-done(((bf16[2048,320]{0,1:T(8,128)(2,1)}), bf16[512,320]{0,1:T(8,128)(2,1)}) %reduce-scatter.26.cloned.1.call-update) | async-done | bytes 327696 | tf_op jit(solution)/shard_map/reduce_scatter | solution.py:289
  990.1 28.1 %reduce-scatter.28.cloned.1.call-done = bf16[512,320]{0,1:T(8,128)(2,1)} async-done(((bf16[2048,320]{0,1:T(8,128)(2,1)}), bf16[512,320]{0,1:T(8,128)(2,1)}) %reduce-scatter.28.cloned.1.call-update) | async-done | bytes 327696 | tf_op jit(solution)/shard_map/reduce_scatter | solution.py:292
  1019.3 23.3 %all_to_all.102 = bf16[512,4,400]{0,2,1:T(8,128)(2,1)S(1)} all-to-all(bf16[512,4,400]{0,2,1:T(8,128)(2,1)S(1)} %bitcast.241), channel_id=1, replica_groups=mesh['row'=8,'col'=4] {'col'}, dimensions={1} | all-to-all | bytes 3276800 | tf_op jit(solution)/shard_map/all_to_all | solution.py:89
  1042.9 5.3 fusion.53
  1049.5 7.9 fusion.51
  1057.5 6.5 fusion.54
  1064.3 7.9 fusion.58
  1072.3 7.9 fusion.56
  1080.3 6.8 fusion.57
  1087.1 30.1 %reduce-scatter.30.cloned.1.call-done = f32[512,960]{0,1:T(8,128)} async-done(((f32[2048,960]{0,1:T(8,128)}), f32[512,960]{0,1:T(8,128)}) %reduce-scatter.30.cloned.1.call-update) | async-done | bytes 1966096 | tf_op jit(solution)/shard_map/reduce_scatter | solution.py:96
  1119.4 69.3 %reduce-scatter.22.cloned.1.call-done = f32[512,960]{0,1:T(8,128)} async-done(((f32[2048,960]{0,1:T(8,128)}), f32[512,960]{0,1:T(8,128)}) %reduce-scatter.22.cloned.1.call-update) | async-done | bytes 1966096 | tf_op jit(solution)/shard_map/reduce_scatter | solution.py:96
  1188.7 4.7 add_convert_fusion
  1195.8 5.7 all-to-all-start.7
  1202.8 38.0 %all-to-all-done.7 = bf16[8,64,960]{2,1,0:T(8,128)(2,1)S(1)} async-done(((bf16[8,64,960]{2,1,0:T(8,128)(2,1)}), bf16[8,64,960]{2,1,0:T(8,128)(2,1)S(1)}, u32[]{:S(2)}, u32[]{:S(2)}) %all-to-all-start.7) | async-done | bytes 983072 | tf_op jit(solution)/shard_map/all_to_all | solution.py:322
  1240.8 3.6 all-to-all-start.3
  1244.4 4.3 fusion.55
  1248.8 31.4 %reduce-scatter.34.cloned.1.call-done = f32[120,400]{1,0:T(8,128)} async-done(((f32[960,400]{1,0:T(8,128)}), f32[120,400]{1,0:T(8,128)}) %reduce-scatter.34.cloned.1.call-update) | async-done | bytes 192016
  1282.0 5.7 all-reduce.4
  1287.7 20.7 %all-reduce.3 = (f32[960]{0:T(1024)}, f32[960]{0:T(1024)}) all-reduce(f32[960]{0:T(1024)S(1)} %get-tuple-element.517, f32[960]{0:T(1024)S(1)} %get-tuple-element.518), channel_id=1, replica_groups=mesh['row'=8,'col'=4] {'row'}, use_global_device_ids=true, to_apply=%region_23.25 | all-reduce | flops 1920 | bytes 15360 | tf_op jit(solution)/shard_map/psum | solution.py:319
  1314.5 39.5 %reduce-scatter.40.cloned.1.call-done = f32[120,640]{1,0:T(8,128)} async-done(((f32[960,640]{1,0:T(8,128)}), f32[120,640]{1,0:T(8,128)}) %reduce-scatter.40.cloned.1.call-update) | async-done | bytes 307216
  1353.9 73.7 %reduce-scatter.36.cloned.1.call-done = f32[120,640]{1,0:T(8,128)} async-done(((f32[960,640]{1,0:T(8,128)}), f32[120,640]{1,0:T(8,128)}) %reduce-scatter.36.cloned.1.call-update) | async-done | bytes 307216
  1427.7 73.8 %reduce-scatter.38.cloned.1.call-done = f32[120,640]{1,0:T(8,128)} async-done(((f32[960,640]{1,0:T(8,128)}), f32[120,640]{1,0:T(8,128)}) %reduce-scatter.38.cloned.1.call-update) | async-done | bytes 307216
  1501.5 66.6 %reduce-scatter.32.cloned.1.call-done = f32[120,240]{1,0:T(8,128)} async-done(((f32[960,240]{1,0:T(8,128)}), f32[120,240]{1,0:T(8,128)}) %reduce-scatter.32.cloned.1.call-update) | async-done | bytes 115216 | tf_op jit(solution)/shard_map/reduce_scatter | solution.py:314
  (415 shorter events, 398.7 us)
Async XLA Ops:
  8.0 74.8 %all-gather.11.cloned.1.call-start = ((), (), s32[]{:S(2)}) async-start(), calls=%async_computation.19 | async-start | bytes 4915200 | tf_op jit(solution)/shard_map/all_gather | solution.py:81
  13.4 33.8 %copy-start.25 = (f32[960]{0:T(1024)S(1)}, f32[960]{0:T(1024)}, u32[]{:S(2)}) copy-start(f32[960]{0:T(1024)} %param.19) | copy-start | bytes 11524
  47.3 366.6 %copy-start = (f32[512,960]{0,1:T(8,128)}, f32[512,960]{0,1:T(8,128)S(1)}, u32[]{:S(2)}) copy-start(f32[512,960]{0,1:T(8,128)S(1)} %copy.93) | copy-start | bytes 5898244
  87.0 5.8 copy-start.29
  88.4 25.2 %all-to-all-start.1 = ((bf16[4,512,400]{1,2,0:T(8,128)(2,1)}), bf16[4,512,400]{1,2,0:T(8,128)(2,1)}, u32[]{:S(2)}, u32[]{:S(2)}) async-start(bf16[4,512,400]{1,2,0:T(8,128)(2,1)} %bitcast.240), calls=%async_computation.1 | async-start | bytes 3276800 | tf_op jit(solution)/shard_map/all_to_all | solution.py:85
  92.7 24.4 %copy-start.32 = (s32[1,3]{1,0:T(1,128)S(1)}, s32[1,3]{1,0:T(1,128)}, u32[]{:S(2)}) copy-start(s32[1,3]{1,0:T(1,128)} %param.27) | copy-start | bytes 40
  92.8 40.0 %all-gather.13.cloned.1.call-start = ((), (), s32[]{:S(2)}) async-start(), calls=%async_computation.20 | async-start | bytes 1638400 | tf_op jit(solution)/shard_map/all_gather | solution.py:228
  93.2 26.9 %copy-start.15 = (f32[512,32]{0,1:T(8,128)}, f32[512,32]{0,1:T(8,128)S(1)}, u32[]{:S(2)}) copy-start(f32[512,32]{0,1:T(8,128)S(1)} %get-tuple-element.542) | copy-start | bytes 196612
  93.2 26.9 %copy-start.17 = (f32[512,32]{0,1:T(8,128)}, f32[512,32]{0,1:T(8,128)S(1)}, u32[]{:S(2)}) copy-start(f32[512,32]{0,1:T(8,128)S(1)} %get-tuple-element.543) | copy-start | bytes 196612
  116.4 36.8 %all-gather.15.cloned.1.call-start = ((), (), s32[]{:S(2)}) async-start(), calls=%async_computation.21 | async-start | bytes 1638400 | tf_op jit(solution)/shard_map/all_gather | solution.py:229
  157.0 149.7 %copy-start.24 = (bf16[120,240]{1,0:T(8,128)(2,1)S(1)}, bf16[120,240]{1,0:T(8,128)(2,1)}, u32[]{:S(2)}) copy-start(bf16[120,240]{1,0:T(8,128)(2,1)} %param.21) | copy-start | bytes 172804
  303.1 35.1 %all-to-all-start.2 = ((bf16[512,4,240]{0,2,1:T(8,128)(2,1)}), bf16[512,4,240]{0,2,1:T(8,128)(2,1)S(1)}, u32[]{:S(2)}, u32[]{:S(2)}) async-start(bf16[512,4,240]{0,2,1:T(8,128)(2,1)} %bitcast.20), calls=%async_computation.2 | async-start | bytes 1966080 | tf_op jit(solution)/shard_map/all_to_all | solution.py:89
  306.6 107.3 %reduce-scatter.20.cloned.1.call-start = ((), (), s32[]{:S(2)}) async-start(), calls=%async_computation.22 | async-start | bytes 9830400 | tf_op jit(solution)/shard_map/reduce_scatter | solution.py:96
  343.5 107.5 %all-gather.21.cloned.1.call-start = ((), (), s32[]{:S(2)}) async-start(), calls=%async_computation.25 | async-start | bytes 1382400 | tf_op jit(solution)/shard_map/all_gather | solution.py:201
  344.1 73.1 %copy-start.23 = (f32[960]{0:T(1024)S(1)}, f32[960]{0:T(1024)}, u32[]{:S(2)}) copy-start(f32[960]{0:T(1024)} %param.22) | copy-start | bytes 11524
  344.1 107.2 %all-gather.17.cloned.1.call-start = ((), (), s32[]{:S(2)}) async-start(), calls=%async_computation.23 | async-start | bytes 4915200 | tf_op jit(solution)/shard_map/all_gather | solution.py:81
  415.8 3.9 copy-start.8
  418.4 76.9 %all-gather.19.cloned.1.call-start = ((), (), s32[]{:S(2)}) async-start(), calls=%async_computation.24 | async-start | bytes 1382400 | tf_op jit(solution)/shard_map/all_gather | solution.py:200
  419.0 119.2 %all-gather.23.cloned.1.call-start = ((), (), s32[]{:S(2)}) async-start(), calls=%async_computation.26 | async-start | bytes 1382400 | tf_op jit(solution)/shard_map/all_gather | solution.py:202
  419.7 153.2 %all-gather.25.cloned.1.call-start = ((), (), s32[]{:S(2)}) async-start(), calls=%async_computation.28 | async-start | bytes 5242880 | tf_op jit(solution)/shard_map/all_gather | solution.py:81
  450.9 210.1 %reduce-scatter.24.cloned.1.call-start = ((), (), s32[]{:S(2)}) async-start(), calls=%async_computation.29 | async-start | bytes 9830400 | tf_op jit(solution)/shard_map/reduce_scatter | solution.py:96
  503.6 79.8 %copy-start.31 = (bf16[960,640]{1,0:T(8,128)(2,1)S(1)}, bf16[960,640]{1,0:T(8,128)(2,1)}, u32[]{:S(2)}) copy-start(bf16[960,640]{1,0:T(8,128)(2,1)} %all-gather.19.cloned.1.call-done) | copy-start | bytes 3686404
  583.4 3.3 copy-start.9
  583.4 3.3 copy-start.19
  592.1 69.0 %copy-start.3 = (f32[512,960]{0,1:T(8,128)S(1)}, f32[512,960]{0,1:T(8,128)}, u32[]{:S(2)}) copy-start(f32[512,960]{0,1:T(8,128)} %copy-done.2) | copy-start | bytes 5898244
  592.1 105.9 %all-gather.27.cloned.1.call-start = ((), (), s32[]{:S(2)}) async-start(), calls=%async_computation.30 | async-start | bytes 4915200 | tf_op jit(solution)/shard_map/all_gather | solution.py:81
  594.6 68.8 %copy-start.6 = (bf16[512,960]{0,1:T(8,128)(2,1)S(1)}, bf16[512,960]{0,1:T(8,128)(2,1)}, u32[]{:S(2)}) copy-start(bf16[512,960]{0,1:T(8,128)(2,1)} %copy.96) | copy-start | bytes 2949124
  702.4 17.2 %all-to-all-start.5 = ((bf16[4,512,240]{1,2,0:T(8,128)(2,1)}), bf16[4,512,240]{1,2,0:T(8,128)(2,1)S(1)}, u32[]{:S(2)}, u32[]{:S(2)}) async-start(bf16[4,512,240]{1,2,0:T(8,128)(2,1)} %bitcast.164), calls=%async_computation.8 | async-start | bytes 1966080 | tf_op jit(solution)/shard_map/all_to_all | solution.py:85
  705.9 283.0 %reduce-scatter.26.cloned.1.call-start = ((), (), s32[]{:S(2)}) async-start(), calls=%async_computation.31 | async-start | bytes 1638400 | tf_op jit(solution)/shard_map/reduce_scatter | solution.py:289
  962.3 56.0 %reduce-scatter.28.cloned.1.call-start = ((), (), s32[]{:S(2)}) async-start(), calls=%async_computation.32 | async-start | bytes 1638400 | tf_op jit(solution)/shard_map/reduce_scatter | solution.py:292
  963.7 153.6 %reduce-scatter.30.cloned.1.call-start = ((), (), s32[]{:S(2)}) async-start(), calls=%async_computation.33 | async-start | bytes 9830400 | tf_op jit(solution)/shard_map/reduce_scatter | solution.py:96
  1019.3 23.6 %copy-start.21 = (bf16[960,400]{0,1:T(8,128)(2,1)S(1)}, bf16[960,400]{0,1:T(8,128)(2,1)}, u32[]{:S(2)}) copy-start(bf16[960,400]{0,1:T(8,128)(2,1)} %reshape.338) | copy-start | bytes 2304004
  1048.3 140.5 %reduce-scatter.22.cloned.1.call-start = ((), (), s32[]{:S(2)}) async-start(), calls=%async_computation.27 | async-start | bytes 9830400 | tf_op jit(solution)/shard_map/reduce_scatter | solution.py:96
  1057.5 222.8 %reduce-scatter.34.cloned.1.call-start = ((), (), s32[]{:S(2)}) async-start(), calls=%async_computation.35 | async-start | bytes 2211840
  1064.0 289.9 %reduce-scatter.40.cloned.1.call-start = ((), (), s32[]{:S(2)}) async-start(), calls=%async_computation.38 | async-start | bytes 2764800
  1072.2 8.1 copy-start.10
  1072.2 355.4 %reduce-scatter.36.cloned.1.call-start = ((), (), s32[]{:S(2)}) async-start(), calls=%async_computation.36 | async-start | bytes 2764800
  1080.2 37.0 %copy-start.26 = (f32[960]{0:T(1024)S(1)}, f32[960]{0:T(1024)}, u32[]{:S(2)}) copy-start(f32[960]{0:T(1024)} %param.19) | copy-start | bytes 11524
  1080.2 37.0 %copy-start.28 = (f32[512]{0:T(512)S(1)}, f32[512]{0:T(512)}, u32[]{:S(2)}) copy-start(f32[512]{0:T(512)} %copy-done.27) | copy-start | bytes 6148
  1080.3 421.2 %reduce-scatter.38.cloned.1.call-start = ((), (), s32[]{:S(2)}) async-start(), calls=%async_computation.37 | async-start | bytes 2764800
  1087.1 30.2 %copy-start.1 = (f32[512,960]{0,1:T(8,128)S(1)}, f32[512,960]{0,1:T(8,128)}, u32[]{:S(2)}) copy-start(f32[512,960]{0,1:T(8,128)} %copy-done) | copy-start | bytes 5898244
  1087.1 101.6 %copy-start.7 = (bf16[512,960]{0,1:T(8,128)(2,1)S(1)}, bf16[512,960]{0,1:T(8,128)(2,1)}, u32[]{:S(2)}) copy-start(bf16[512,960]{0,1:T(8,128)(2,1)} %copy.96) | copy-start | bytes 2949124
  1193.5 8.0 copy-start.13
  1195.8 48.6 %copy-start.12 = (bf16[4,30,8,512]{3,2,0,1:T(8,128)(2,1)S(1)}, bf16[4,30,8,512]{3,2,0,1:T(8,128)(2,1)}, u32[]{:S(2)}) copy-start(bf16[4,30,8,512]{3,2,0,1:T(8,128)(2,1)} %copy-done.11) | copy-start | bytes 2949124
  1195.8 44.9 %all-to-all-start.7 = ((bf16[8,64,960]{2,1,0:T(8,128)(2,1)}), bf16[8,64,960]{2,1,0:T(8,128)(2,1)S(1)}, u32[]{:S(2)}, u32[]{:S(2)}) async-start(bf16[8,64,960]{2,1,0:T(8,128)(2,1)} %bitcast.42), calls=%async_computation.13 | async-start | bytes 2097152 | tf_op jit(solution)/shard_map/all_to_all | solution.py:322
  1240.8 68.3 %all-to-all-start.3 = ((bf16[8,64,960]{2,1,0:T(8,128)(2,1)}), bf16[8,64,960]{2,1,0:T(8,128)(2,1)S(1)}, u32[]{:S(2)}, u32[]{:S(2)}) async-start(bf16[8,64,960]{2,1,0:T(8,128)(2,1)} %bitcast.22), calls=%async_computation.5 | async-start | bytes 2097152 | tf_op jit(solution)/shard_map/all_to_all | solution.py:321
  1244.3 4.4 copy-start.33
  1244.3 323.8 %reduce-scatter.32.cloned.1.call-start = ((), (), s32[]{:S(2)}) async-start(), calls=%async_computation.34 | async-start | bytes 1105920 | tf_op jit(solution)/shard_map/reduce_scatter | solution.py:314
  (12 other events, 19.8 us)
Sparse Core Ops, SparseCore 0:
  48.8 32.0 all-gather.10
  116.5 16.2 all-gather.12
  134.9 18.1 all-gather.14
  343.6 70.1 reduce-scatter.19
  665.0 32.9 all-gather.26
  962.4 26.5 reduce-scatter.25
  991.7 26.5 reduce-scatter.27
Sparse Core Ops, SparseCore 1:
  346.1 42.9 all-gather.20
  418.5 32.8 all-gather.16
  453.6 41.7 all-gather.18
  497.8 40.4 all-gather.22
  539.9 33.0 all-gather.24
  592.2 68.8 reduce-scatter.23
  1048.3 68.9 reduce-scatter.29
  1119.8 68.8 reduce-scatter.21
  1192.1 88.1 reduce-scatter.33
  1284.9 69.0 reduce-scatter.39
  1358.5 69.2 reduce-scatter.35
  1432.3 69.1 reduce-scatter.37
  1505.6 62.4 reduce-scatter.31
